TPU v7x, 256 devices: a whole 4x4x8 slice. The times are simulated.
256 devices in a mesh: ctx: 64 (over z, x, core), head: 4 (over y).
Axes of the slice: x: 4, y: 4, z: 8, core: 2. Of those that a mesh axis runs over, the one named last changes fastest.
Arguments:
- queries: bfloat16 [65536, 1024], P('ctx', 'head'), may hold values from -6 to 6
- keys: bfloat16 [65536, 1024], P('ctx', 'head'), may hold values from -6 to 6
- values: bfloat16 [65536, 1024], P('ctx', 'head'), may hold values from -6 to 6
- level_index: int32 [65536], P('ctx'), may hold values from 0 to 15
- level_table: float32 [16, 8, 11], P(None, 'head'), may hold values from 0.2 to 2
- head_gain: float32 [1024], P('head'), may hold values from 0.5 to 1.5
- residual: bfloat16 [65536, 1024], P(('ctx', 'head')), may hold values from -6 to 6
- w_out: bfloat16 [1024, 1024], replicated, may hold values from -0.1875 to 0.1875
- norm_gain: float32 [1024], replicated, may hold values from 0.5 to 1.5
- w_qkv: bfloat16 [1024, 3072], replicated, may hold values from -8 to 8
- windows: int32 [8], replicated, may hold values from 64 to 256, as said below
Outputs:
- hidden: bfloat16 [65536, 1024], P(('ctx', 'head'))
- attended: bfloat16 [65536, 1024], P('ctx', 'head')
Inputs may be any that keep to these rules, and one draw needn't show every extreme that they name: `windows`: each head's key window; some head's window is exactly 256 in every draw.
All inputs are finite; a program needn't handle non-finite values.
Results may differ from a plain program's by a relative error of at most 0.014.
Values may be sent and summed in bfloat16 or wider, within the bound.
No kernel may reach another device: no remote copies, remote signals or barrier semaphores. Data moves between devices by JAX's collectives and lax.ppermute only.
A program may use at most 128 MiB of HBM per device.

v0:
```python
import jax
import jax.numpy as jnp
from jax import lax
from jax.sharding import PartitionSpec as P

STRETCH = 64
WINDOW = 256


EPSILON = 1e-05
PRECISE = lax.Precision.HIGHEST


def from_behind(block, axis, distance):
    devices = range(lax.axis_size(axis))
    route = [(i - distance, i) for i in devices if i - distance in devices]
    return lax.ppermute(block, axis, route)


def bfloat(array):
    return array.astype(jnp.bfloat16)


def attend_block(
    query_block, key_block, value_block, head_windows, query_pos, key_pos, score_scale
):
    scores = (
        jnp.einsum("qhd,khd->hqk", query_block, key_block, preferred_element_type=jnp.float32)
        * score_scale
    )
    distance = query_pos[:, None] - key_pos[None, :]
    allowed = (
        (distance >= 0)[None]
        & (distance < head_windows[:, None, None])
        & (key_pos >= 0)[None, None, :]
    )
    scores = jnp.where(allowed, scores, -1e30)
    row_max = jnp.max(scores, -1, keepdims=True)
    weights = jnp.exp(scores - row_max)
    probs = bfloat(weights / jnp.sum(weights, -1, keepdims=True))
    return bfloat(
        jnp.einsum("hqk,khd->qhd", probs, value_block, preferred_element_type=jnp.float32)
    )


def windowed(query_rows, key_value, head_windows, first_pos, context_rows, score_scale):
    query_count = query_rows.shape[0]
    block_rows = min(query_count, 512)
    block_count = query_count // block_rows

    def attend_one(block_index):
        offset = block_index * block_rows
        query_block = lax.dynamic_slice_in_dim(query_rows, offset, block_rows, 0)
        pair_block = lax.dynamic_slice_in_dim(key_value, offset, context_rows + block_rows, 0)
        query_pos = first_pos + offset + jnp.arange(block_rows, dtype=jnp.int32)
        key_pos = (
            first_pos
            + offset
            - context_rows
            + jnp.arange(context_rows + block_rows, dtype=jnp.int32)
        )
        return attend_block(
            query_block,
            pair_block[:, 0],
            pair_block[:, 1],
            head_windows,
            query_pos,
            key_pos,
            score_scale,
        )

    results = lax.map(attend_one, jnp.arange(block_count, dtype=jnp.int32))
    return results.reshape((query_count,) + query_rows.shape[1:])


def per_device(
    queries,
    keys,
    values,
    level_index,
    level_table,
    head_gain,
    residual,
    w_out,
    norm_gain,
    w_qkv,
    windows,
):
    token_count = queries.shape[0]
    local_heads = level_table.shape[1]
    levels = level_table.shape[2]
    head_dim = head_gain.shape[0] // local_heads
    stretch_len = STRETCH
    stretches = token_count // stretch_len
    local_bits = stretches.bit_length() - 1
    ctx_bits = lax.axis_size("ctx").bit_length() - 1
    position = lax.axis_index("ctx")
    stretch_shape = (stretches, stretch_len, local_heads, head_dim)
    query_stretches = queries.reshape(stretch_shape)
    key_stretches = keys.reshape(stretch_shape)
    value_stretches = values.reshape(stretch_shape)
    states = jnp.einsum(
        "jchd,jche->jhde", key_stretches, value_stretches, preferred_element_type=jnp.float32
    )
    device_state = jnp.sum(states, 0).reshape(local_heads * head_dim, head_dim)
    piece = lax.all_gather(device_state[None], "ctx", axis=0, tiled=True)
    piece_rows = piece.shape[0]
    source = jnp.arange(piece_rows, dtype=jnp.int32)
    span_sizes = 2 ** jnp.arange(ctx_bits, dtype=jnp.int32)
    lower_edge = position // (2 * span_sizes) * (2 * span_sizes)
    upper_edge = position // span_sizes * span_sizes
    member = ((source[:, None] >= lower_edge[None]) & (source[:, None] < upper_edge[None])).astype(
        jnp.float32
    )
    remote = jnp.einsum("nb,nxy->bxy", member, piece, precision=PRECISE)
    level_rows = level_table.reshape(level_table.shape[0], local_heads * levels)
    onehot = (
        level_index[:, None] == jnp.arange(level_rows.shape[0], dtype=jnp.int32)[None]
    ).astype(jnp.float32)
    level_weight = jnp.dot(onehot, level_rows, precision=PRECISE).reshape(
        stretches, stretch_len, local_heads, levels
    )
    causal = (
        jnp.arange(stretch_len, dtype=jnp.int32)[:, None]
        >= jnp.arange(stretch_len, dtype=jnp.int32)[None, :]
    )
    scores = jnp.einsum(
        "jthd,jshd->jhts", query_stretches, key_stretches, preferred_element_type=jnp.float32
    )
    scores = bfloat(jnp.where(causal[None, None], scores, 0.0))
    inside = jnp.einsum(
        "jhts,jshd->jthd", scores, value_stretches, preferred_element_type=jnp.float32
    )
    running = level_weight[..., 0:1] * stretch_len ** (-0.5) * inside
    for level_bit in range(local_bits):
        block_len = 2**level_bit
        group_total = stretches // block_len
        grouped = jnp.sum(
            states.reshape(group_total, block_len, local_heads, head_dim, head_dim), 1
        )
        earlier = jnp.concatenate([jnp.zeros_like(grouped[:1]), grouped[:-1]], 0)
        odd_mask = (jnp.arange(group_total, dtype=jnp.int32) % 2).astype(jnp.float32)
        read_state = bfloat(earlier * odd_mask[:, None, None, None])
        blocked_query = query_stretches.reshape(
            group_total, block_len * stretch_len, local_heads, head_dim
        )
        part_sum = jnp.einsum(
            "mthd,mhde->mthe", blocked_query, read_state, preferred_element_type=jnp.float32
        )
        weight_now = level_weight[..., 1 + level_bit : 2 + level_bit] * (
            stretch_len * block_len
        ) ** (-0.5)
        running = running + weight_now * part_sum.reshape(stretch_shape)
    remote_read = bfloat(remote.reshape(ctx_bits, local_heads, head_dim, head_dim))
    flat_query = queries.reshape(token_count, local_heads, head_dim)
    far_terms = jnp.einsum(
        "thd,bhde->tbhe", flat_query, remote_read, preferred_element_type=jnp.float32
    )
    far_rates = jnp.array(
        [(stretch_len * 2 ** (local_bits + level_bit)) ** (-0.5) for level_bit in range(ctx_bits)],
        jnp.float32,
    )
    far_weights = (
        level_weight.reshape(token_count, local_heads, levels)[:, :, 1 + local_bits :] * far_rates
    )
    running = running.reshape(token_count, local_heads, head_dim) + jnp.einsum(
        "tbhe,thb->the", far_terms, far_weights, precision=PRECISE
    )
    mean_square = jnp.mean(running * running, -1, keepdims=True)
    heads_out = bfloat(
        running * lax.rsqrt(mean_square + EPSILON) * head_gain.reshape(local_heads, head_dim)
    )
    group_count = lax.axis_size("head")
    row_count = token_count // group_count
    sectioned = heads_out.reshape(group_count, row_count, local_heads * head_dim)
    projected = jnp.einsum(
        "grc,cd->grd",
        lax.all_to_all(sectioned, "head", split_axis=0, concat_axis=2, tiled=True),
        w_out,
        preferred_element_type=jnp.float32,
    )
    hidden = bfloat(residual.astype(jnp.float32) + projected[0])
    hidden_f = hidden.astype(jnp.float32)
    normed = bfloat(
        hidden_f * lax.rsqrt(jnp.mean(hidden_f * hidden_f, -1, keepdims=True) + EPSILON) * norm_gain
    )
    projected_qkv = bfloat(jnp.dot(normed, w_qkv, preferred_element_type=jnp.float32))
    score_scale = head_dim ** (-0.5)
    split_qkv = projected_qkv.reshape(row_count, 3, group_count, local_heads * head_dim)
    local_qkv = lax.all_to_all(split_qkv, "head", split_axis=2, concat_axis=0, tiled=True)
    local_qkv = local_qkv.reshape(token_count, 3, local_heads, head_dim)
    tail_len = min(token_count, WINDOW)
    need_count = (WINDOW - 1 + token_count - 1) // token_count
    tail_pairs = local_qkv[token_count - tail_len :, 1:3]
    before = [from_behind(tail_pairs, "ctx", 1)]
    key_value = jnp.concatenate(before + [local_qkv[:, 1:3]], 0)
    head_windows = lax.dynamic_slice_in_dim(
        windows, lax.axis_index("head") * local_heads, local_heads
    )
    first_pos = position * token_count
    result = windowed(
        local_qkv[:, 0], key_value, head_windows, first_pos, need_count * tail_len, score_scale
    )
    return (hidden, result.reshape(token_count, local_heads * head_dim))


def solution(mesh):
    in_specs = (
        P("ctx", "head"),
        P("ctx", "head"),
        P("ctx", "head"),
        P("ctx"),
        P(None, "head", None),
        P("head"),
        P(("ctx", "head"), None),
        P(),
        P(),
        P(),
        P(),
    )
    out_specs = (P(("ctx", "head"), None), P("ctx", "head"))
    return jax.shard_map(
        per_device, mesh=mesh, in_specs=in_specs, out_specs=out_specs, check_vma=False
    )
```

profile of v0, /device:TPU:7, one launch (start us, length us, event | category | flops | bytes accessed | tf_op | source)
XLA Modules:
  0.0 228.7 jit_solution(5243764467069019587)
XLA Ops:
  8.5 2.0 reshape.270
  10.6 3.6 %fusion.96 = (f32[2,128,128]{2,1,0:T(8,128)}, f32[16,2,128,128]{3,2,1,0:T(8,128)}) fusion(bf16[16,64,2,128]{3,2,1,0:T(2,128)(2,1)} %reshape.270, bf16[16,64,2,128]{3,2,1,0:T(2,128)(2,1)S(1)} %reshape.269), kind=kOutput, calls=%fused_computation.147 | convolution fusion | flops 67600384 | bytes 3276800 | tf_op jit(solution)/shard_map/jchd,jche->jhde/dot_general | solution.py:102
  19.6 3.2 %slice.68 = f32[15,2,128,128]{3,2,1,0:T(8,128)} slice(f32[16,2,128,128]{3,2,1,0:T(8,128)} %get-tuple-element.135), slice={[0:15], [0:2], [0:128], [0:128]} | slice | bytes 3932160 | tf_op jit(solution)/shard_map/slice | solution.py:141
  26.4 1.4 convolution_bitcast_fusion.2
  27.8 2.6 %copy.101 = f32[4,256,2,128]{3,1,0,2:T(8,128)} copy(f32[4,256,2,128]{1,3,2,0:T(8,128)} %convolution_bitcast_fusion.2) | data formatting | bytes 2097152 | tf_op jit(solution)/shard_map/mthd,mhde->mthe/transpose | solution.py:147
  30.4 1.7 bitcast_reduce_fusion
  33.6 2.6 %copy.106 = f32[2,512,2,128]{3,1,0,2:T(8,128)} copy(f32[2,512,2,128]{1,3,2,0:T(8,128)} %convolution_bitcast_fusion.1) | data formatting | bytes 2097152 | tf_op jit(solution)/shard_map/mthd,mhde->mthe/transpose | solution.py:147
  36.3 3.2 %fusion.36 = f32[16,64,2,128]{3,1,2,0:T(8,128)} fusion(f32[15,2,128,128]{3,2,1,0:T(8,128)} %slice.68, f32[16]{0:T(128)S(1)} %fusion.84, f32[16,64,2]{1,2,0:T(2,128)S(1)} %copy.90, bf16[16,64,2,128]{3,2,1,0:T(2,128)(2,1)} %reshape.268), kind=kOutput, calls=%fused_computation.54 | convolution fusion | flops 68419584 | bytes 3547200 | tf_op jit(solution)/shard_map/mthd,mhde->mthe/dot_general | solution.py:147
  39.5 4.6 %fusion.35 = f32[16,64,2,128]{3,1,2,0:T(8,128)} fusion(f32[16,64,2,128]{3,1,2,0:T(8,128)} %fusion.36, f32[16,64,2,128]{3,1,0,2:T(8,128)} %bitcast.120, f32[16,64,2,128]{3,1,0,2:T(8,128)} %bitcast.119, f32[16,64,2,128]{3,1,0,2:T(8,128)} %bitcast.118, f32[16,64,2]{1,2,0:T(2,128)S(1)} %copy.103, f32[16,64,2]{1,2,0:T(2,128)S(1)} %copy.98, ...), kind=kOutput, calls=%fused_computation.52 | convolution fusion | flops 69468160 | bytes 6852608 | tf_op jit(solution)/shard_map/jhts,jshd->jthd/dot_general | solution.py:131
  45.7 53.0 %all-gather.2.cloned.1.call-done = f32[64,256,128]{2,1,0:T(8,128)} async-done(((f32[1,256,128]{2,1,0:T(8,128)}), f32[64,256,128]{2,1,0:T(8,128)}) %all-gather.2.cloned.1.call-update) | async-done | bytes 8388624 | tf_op jit(solution)/shard_map/all_gather | solution.py:106
  98.7 10.7 %fusion.39 = bf16[6,256,128]{2,0,1:T(8,128)(2,1)S(1)} fusion(f32[64,256,128]{2,1,0:T(8,128)} %all-gather.2.cloned.1.call-done, s32[6]{0:T(128)S(1)} %get-tuple-element.138, s32[6]{0:T(128)S(1)} %get-tuple-element.139), kind=kOutput, calls=%fused_computation.61 | convolution fusion | flops 151192704 | bytes 8781872 | tf_op jit(solution)/shard_map/nb,nxy->bxy/dot_general | solution.py:115
  109.4 2.0 fusion.30
  111.4 2.6 %copy.129 = f32[1024,2,128]{2,0,1:T(8,128)} copy(f32[1024,2,128]{0,2,1:T(8,128)} %fusion.30) | data formatting | bytes 2097152 | tf_op jit(solution)/shard_map/tbhe,thb->the/dot_general | solution.py:166
  114.0 1.7 multiply_reduce_fusion
  117.0 12.8 %all_to_all.30 = bf16[4,256,256]{2,1,0:T(8,128)(2,1)S(1)} all-to-all(bf16[4,256,256]{2,1,0:T(8,128)(2,1)S(1)} %reshape.279), channel_id=1, replica_groups=mesh['ctx'=64,'head'=4] {'head'}, dimensions={0} | all-to-all | bytes 1048576 | tf_op jit(solution)/shard_map/all_to_all | solution.py:178
  130.1 1.9 fusion.42
  132.8 5.8 %convolution_convert_fusion = bf16[256,3072]{1,0:T(8,128)(2,1)} fusion(bf16[1024,3072]{1,0:T(8,128)(2,1)} %param.23, bf16[256,1024]{1,0:T(8,128)(2,1)S(1)} %get-tuple-element.137, f32[1024]{0:T(1024)S(1)} %copy-done.15, f32[256]{0:T(256)S(1)} %add_rsqrt_fusion.1), kind=kOutput, calls=%fused_computation.38 | convolution fusion | flops 1612447744 | bytes 8393728 | tf_op jit(solution)/shard_map/dot_general | solution.py:187
  138.6 4.2 %reshape.281 = bf16[256,3,4,256]{3,2,1,0:T(4,128)(2,1)} reshape(bf16[256,3072]{1,0:T(8,128)(2,1)} %convolution_convert_fusion) | data formatting | bytes 3145728 | tf_op jit(solution)/shard_map/reshape | solution.py:189
  142.8 1.6 copy.114
  144.5 21.6 %all_to_all.31 = bf16[256,3,4,256]{3,0,1,2:T(8,128)(2,1)S(1)} all-to-all(bf16[256,3,4,256]{3,0,1,2:T(8,128)(2,1)S(1)} %copy.114), channel_id=1, replica_groups=mesh['ctx'=64,'head'=4] {'head'}, dimensions={2} | all-to-all | bytes 3145728 | tf_op jit(solution)/shard_map/all_to_all | solution.py:190
  167.3 3.5 %reshape.282 = bf16[1024,3,2,128]{3,2,0,1:T(2,128)(2,1)} reshape(bf16[4,256,3,1,256]{4,1,0,2,3:T(8,128)(2,1)} %copy.115) | data formatting | bytes 3145728 | tf_op jit(solution)/shard_map/reshape | solution.py:191
  170.8 1.9 slice.76
  172.8 7.3 %collective-permute-start = (bf16[256,2,2,128]{3,2,0,1:T(2,128)(2,1)}, bf16[256,2,2,128]{3,2,0,1:T(2,128)(2,1)S(1)}, u32[]{:S(2)}, u32[]{:S(2)}) collective-permute-start(bf16[256,2,2,128]{3,2,0,1:T(2,128)(2,1)} %slice.76), channel_id=1, source_target_pairs={{0,4},{4,8},{8,12},{12,16},{16,20},{20,24},{24,28},{28,32},{32,36}... | collective-permute-start | bytes 786440 | tf_op jit(solution)/shard_map/ppermute | solution.py:17
  183.5 5.2 %pad_maximum_fusion = bf16[1280,2,2,128]{3,2,0,1:T(2,128)(2,1)} fusion(bf16[1024,2,2,128]{3,2,0,1:T(2,128)(2,1)S(1)} %slice-done, bf16[256,2,2,128]{3,2,0,1:T(2,128)(2,1)S(1)} %collective-permute-done), kind=kLoop, calls=%fused_computation.58 | loop fusion | flops 655360 | bytes 2621440 | tf_op jit(solution)/shard_map/concatenate | solution.py:196
  188.7 31.2 %while.12 = (s32[]{:T(128)}, bf16[2,512,2,128]{3,2,1,0:T(2,128)(2,1)}, s32[2]{0:T(128)S(1)}, bf16[1280,2,2,128]{3,2,0,1:T(2,128)(2,1)}, s32[]{:T(128)}, /*index=...) while((s32[]{:T(128)}, ...), condition=%wide.region_9.10_spmd, body=%wide.region_6.9_spmd.sunk | while | flops 617092352 | bytes 11036708 | solution.py:72
  189.9 1.7 constant_dynamic-slice_fusion.5
  194.4 3.0 %fusion.107 = f32[2,512]{1,0:T(2,128)S(1)} fusion(s32[512,768]{1,0:T(8,128)} %broadcast_subtract_fusion.2, s32[2]{0:T(128)S(1)} %get-tuple-element.220, pred[768]{0:T(1024)(128)(4,1)S(1)} %broadcast_compare_fusion.4, pred[512,768]{1,0:T(8,128)(4,1)S(1)} %broadcast_compare_fusion.5, bf16[768,1,2,128]{3,2,0,1:T(2,128)(2,1)S(1)} %get-tuple-element.185, ...), kind=kOutput, calls=%fused_computation.146.clone.1 | convolution fusion | flops 206832384 | bytes 2626312 | tf_op jit(solution)/shard_map/while/body/eval_jaxpr/sub | solution.py:39
  197.4 4.9 %fusion.108 = bf16[1,512,2,128]{1,3,2,0:T(8,128)(2,1)} fusion(f32[2,512]{1,0:T(2,128)S(1)} %fusion.107, bf16[768,1,2,128]{3,2,0,1:T(2,128)(2,1)S(1)} %get-tuple-element.186, s32[512,768]{1,0:T(8,128)} %broadcast_subtract_fusion.2, s32[2]{0:T(128)S(1)} %get-tuple-element.220, pred[768]{0:T(1024)(128)(4,1)S(1)} %broadcast_compare_fusion.4, ...), kind=kOutput, calls=%fused_computation.13.clone.1 | convolution fusion | flops 409077504 | bytes 3281672 | tf_op jit(solution)/shard_map/while/body/eval_jaxpr/hqk,khd->qhd/dot_general | solution.py:42
  205.5 1.7 constant_dynamic-slice_fusion.5
  210.0 3.0 %fusion.107 = f32[2,512]{1,0:T(2,128)S(1)} fusion(s32[512,768]{1,0:T(8,128)} %broadcast_subtract_fusion.2, s32[2]{0:T(128)S(1)} %get-tuple-element.220, pred[768]{0:T(1024)(128)(4,1)S(1)} %broadcast_compare_fusion.4, pred[512,768]{1,0:T(8,128)(4,1)S(1)} %broadcast_compare_fusion.5, bf16[768,1,2,128]{3,2,0,1:T(2,128)(2,1)S(1)} %get-tuple-element.185, ...), kind=kOutput, calls=%fused_computation.146.clone.1 | convolution fusion | flops 206832384 | bytes 2626312 | tf_op jit(solution)/shard_map/while/body/eval_jaxpr/sub | solution.py:39
  213.0 4.9 %fusion.108 = bf16[1,512,2,128]{1,3,2,0:T(8,128)(2,1)} fusion(f32[2,512]{1,0:T(2,128)S(1)} %fusion.107, bf16[768,1,2,128]{3,2,0,1:T(2,128)(2,1)S(1)} %get-tuple-element.186, s32[512,768]{1,0:T(8,128)} %broadcast_subtract_fusion.2, s32[2]{0:T(128)S(1)} %get-tuple-element.220, pred[768]{0:T(1024)(128)(4,1)S(1)} %broadcast_compare_fusion.4, ...), kind=kOutput, calls=%fused_computation.13.clone.1 | convolution fusion | flops 409077504 | bytes 3281672 | tf_op jit(solution)/shard_map/while/body/eval_jaxpr/hqk,khd->qhd/dot_general | solution.py:42
  219.9 1.9 copy.207
  (101 shorter events, 31.0 us)
Async XLA Ops:
  7.2 122.9 %copy-start = (bf16[1024,1024]{1,0:T(8,128)(2,1)S(1)}, bf16[1024,1024]{1,0:T(8,128)(2,1)}, u32[]{:S(2)}) copy-start(bf16[1024,1024]{1,0:T(8,128)(2,1)} %param.21) | copy-start | bytes 6291460
  7.2 91.6 %all-gather.2.cloned.1.call-start = ((), (), s32[]{:S(2)}) async-start(), calls=%async_computation.2 | async-start | bytes 8519680 | tf_op jit(solution)/shard_map/all_gather | solution.py:106
  8.5 5.6 %copy-start.2 = (bf16[1024,256]{1,0:T(8,128)(2,1)S(1)}, bf16[1024,256]{1,0:T(8,128)(2,1)}, u32[]{:S(2)}) copy-start(bf16[1024,256]{1,0:T(8,128)(2,1)} %param.14) | copy-start | bytes 1572868
  14.2 3.7 %copy-start.11 = (f32[16,2,11]{0,1,2:T(2,128)S(1)}, f32[16,2,11]{0,1,2:T(2,128)}, u32[]{:S(2)}) copy-start(f32[16,2,11]{0,1,2:T(2,128)} %param.18) | copy-start | bytes 4228
  14.2 3.9 %copy-start.14 = (s32[1024]{0:T(1024)S(1)}, s32[1024]{0:T(1024)}, u32[]{:S(2)}) copy-start(s32[1024]{0:T(1024)} %param.17) | copy-start | bytes 12292
  19.6 3.2 %copy-start.1 = (f32[16,2,128,128]{3,2,1,0:T(8,128)S(1)}, f32[16,2,128,128]{3,2,1,0:T(8,128)}, u32[]{:S(2)}) copy-start(f32[16,2,128,128]{3,2,1,0:T(8,128)} %get-tuple-element.135) | copy-start | bytes 6291460
  22.8 1.0 copy-start.8
  25.4 1.0 copy-start.6
  27.8 4.4 %copy-start.7 = (bf16[2,512,2,128]{3,2,1,0:T(2,128)(2,1)S(1)}, bf16[2,512,2,128]{3,2,1,0:T(2,128)(2,1)}, u32[]{:S(2)}) copy-start(bf16[2,512,2,128]{3,2,1,0:T(2,128)(2,1)} %reshape_reshape.17) | copy-start | bytes 1572868
  36.2 3.3 %copy-start.5 = (bf16[16,64,2,128]{3,2,1,0:T(2,128)(2,1)S(1)}, bf16[16,64,2,128]{3,2,1,0:T(2,128)(2,1)}, u32[]{:S(2)}) copy-start(bf16[16,64,2,128]{3,2,1,0:T(2,128)(2,1)} %reshape.270) | copy-start | bytes 1572868
  44.2 1.5 copy-start.13
  98.7 10.7 %copy-start.9 = (bf16[1024,2,128]{2,1,0:T(2,128)(2,1)S(1)}, bf16[1024,2,128]{2,1,0:T(2,128)(2,1)}, u32[]{:S(2)}) copy-start(bf16[1024,2,128]{2,1,0:T(2,128)(2,1)} %reshape.278) | copy-start | bytes 1572868
  111.4 4.3 %copy-start.12 = (f32[256]{0:T(256)S(1)}, f32[256]{0:T(256)}, u32[]{:S(2)}) copy-start(f32[256]{0:T(256)} %param.19) | copy-start | bytes 3076
  114.0 1.7 copy-start.3
  130.1 2.7 %copy-start.15 = (f32[1024]{0:T(1024)S(1)}, f32[1024]{0:T(1024)}, u32[]{:S(2)}) copy-start(f32[1024]{0:T(1024)} %param.22) | copy-start | bytes 12292
  132.0 0.8 copy-start.10
  167.3 12.8 %copy-start.16 = (s32[8]{0:T(128)S(1)}, s32[8]{0:T(128)}, u32[]{:S(2)}) copy-start(s32[8]{0:T(128)} %param.24) | copy-start | bytes 100
  170.8 12.6 %slice-start = ((bf16[1024,3,2,128]{3,2,0,1:T(2,128)(2,1)}), bf16[1024,2,2,128]{3,2,0,1:T(2,128)(2,1)S(1)}, s32[]{:S(2)}) async-start(bf16[1024,3,2,128]{3,2,0,1:T(2,128)(2,1)} %reshape.282), calls=%async_computation.3 | async-start | bytes 2097152 | tf_op jit(solution)/shard_map/slice | solution.py:196
  172.8 10.7 %collective-permute-start = (bf16[256,2,2,128]{3,2,0,1:T(2,128)(2,1)}, bf16[256,2,2,128]{3,2,0,1:T(2,128)(2,1)S(1)}, u32[]{:S(2)}, u32[]{:S(2)}) collective-permute-start(bf16[256,2,2,128]{3,2,0,1:T(2,128)(2,1)} %slice.76), channel_id=1, source_target_pairs={{0,4},{4,8},{8,12},{12,16},{16,20},{20,24},{24,28},{28,32},{32,36}... | collective-permute-start | bytes 786440 | tf_op jit(solution)/shard_map/ppermute | solution.py:17
  180.1 1.4 copy-start.4
Sparse Core Ops, SparseCore 0:
  14.3 84.3 all-gather.1
where the time goes:
time: 232 us; the launch traced here: 229 us
  waiting for transfers between devices  53.8 us (23%)
  local copies, waits for them, and re-layouts  53.2 us (23%)
  matrix products  51.3 us (22%)
  blocking collectives  34.4 us (15%)
  between operations  14.4 us (6%)
  other arithmetic  12.9 us (6%)
  starting transfers between devices  7.34 us (3%)
    all_gather x1, waiting for transfers between devices, per_device(): piece = lax.all_gather(device_state[None], 'ctx', axis=0, tiled=True)  53 us
    all_to_all x1, blocking collectives, per_device(): lax.all_to_all(split_qkv, 'head', split_axis=2, concat_axis=0, tiled=True)  21.6 us
    all_to_all x1, blocking collectives, per_device(): lax.all_to_all(sectioned, 'head', split_axis=0, concat_axis=2, tiled=True)  12.8 us
    dot_general x1, matrix products, per_device(): remote = jnp.einsum('nb,nxy->bxy', member, piece, precision=PRECISE)  10.7 us
    dot_general x2, matrix products, attend_block(): jnp.einsum('hqk,khd->qhd', probs, value_block, preferred_element_type=jnp...  9.72 us
    ppermute x1, starting transfers between devices, from_behind(): return lax.ppermute(block, axis, route)  7.3 us
    dot_general x4, matrix products, per_device(): jnp.einsum('mthd,mhde->mthe', blocked_query, read_state, preferred_elemen...  6.39 us
    transpose x3, local copies, waits for them, and re-layouts, per_device(): jnp.einsum('mthd,mhde->mthe', blocked_query, read_state, preferred_elemen...  6.37 us
  transfers between devices with their start and end apart: 2, of which 2 were waited for; matrix products, arithmetic and copies ran while one was open for 13% of the time, Pallas kernels for 0%

commit v1 on v0

v1 whole, which is shorter than its diff:
```python
import jax
import jax.numpy as jnp
from jax import lax
from jax.experimental import pallas as pl
from jax.experimental.pallas import tpu as pltpu
from jax.sharding import PartitionSpec as P

STRETCH = 64
WINDOW = 256
EPSILON = 1e-05
BLOCK = 256
DH = 128
CTX_ROUTES = (1, 2, 6, 8, 16, 48)

VMEM = pl.BlockSpec(memory_space=pltpu.VMEM)
SMEM = pl.BlockSpec(memory_space=pltpu.SMEM)
F32 = jnp.float32
BF16 = jnp.bfloat16


def dot(a, b, dims=((1,), (0,))):
    return lax.dot_general(a, b, (dims, ((), ())), preferred_element_type=F32)


def call(kernel, outs, args, specs, flops, nbytes, name, vmem=24):
    return pl.pallas_call(
        kernel,
        out_shape=[jax.ShapeDtypeStruct(s, d) for s, d in outs],
        in_specs=specs,
        out_specs=[VMEM] * len(outs),
        compiler_params=pltpu.CompilerParams(vmem_limit_bytes=vmem * 2**20),
        cost_estimate=pl.CostEstimate(flops=flops, bytes_accessed=nbytes, transcendentals=0),
        name=name,
    )(*args)


def state_kernel(k_ref, v_ref, state_ref, send_ref, read_ref):
    heads = state_ref.shape[0] // DH
    for h in range(heads):
        lanes = slice(h * DH, (h + 1) * DH)
        blocks = []
        for i in range(k_ref.shape[0] // BLOCK):
            rows = slice(i * BLOCK, (i + 1) * BLOCK)
            blocks.append(dot(k_ref[rows, lanes], v_ref[rows, lanes], ((0,), (0,))))
        half = blocks[0] + blocks[1]
        total = half + (blocks[2] + blocks[3])
        state_ref[lanes, :] = total
        send_ref[lanes, :] = total.astype(BF16)
        read_ref[0, lanes, :] = blocks[0].astype(BF16)
        read_ref[1, lanes, :] = blocks[2].astype(BF16)
        read_ref[2, lanes, :] = half.astype(BF16)


def weight_kernel(index_ref, table_ref, weight_ref):
    table = table_ref[...]
    high = table.astype(BF16)
    rest = table - high.astype(F32)
    middle = rest.astype(BF16)
    low = (rest - middle.astype(F32)).astype(BF16)
    pieces = jnp.concatenate([high, middle, low], 0)
    index = index_ref[...]
    rows = lax.broadcasted_iota(jnp.int32, (table.shape[0], index.shape[1]), 0)
    onehot = (rows == index).astype(F32).astype(BF16)
    weight_ref[...] = dot(jnp.concatenate([onehot] * 3, 0), pieces, ((0,), (0,)))


def local_kernel(levels, q_ref, k_ref, v_ref, read_ref, weight_ref, run_ref):
    heads = run_ref.shape[1] // DH
    t = lax.broadcasted_iota(jnp.int32, (BLOCK, BLOCK), 0)
    s = lax.broadcasted_iota(jnp.int32, (BLOCK, BLOCK), 1)
    same = t // STRETCH == s // STRETCH
    pair = t // (2 * STRETCH) == s // (2 * STRETCH)
    causal = t >= s
    for i in range(q_ref.shape[0] // BLOCK):
        rows = slice(i * BLOCK, (i + 1) * BLOCK)
        for h in range(heads):
            lanes = slice(h * DH, (h + 1) * DH)
            q = q_ref[rows, lanes]

            def weight(level):
                c = h * levels + level
                return weight_ref[rows, c : c + 1]

            scores = dot(q, k_ref[rows, lanes], ((1,), (1,)))
            scale = jnp.where(same, weight(0), jnp.where(pair, weight(1), weight(2)))
            mixed = jnp.where(causal, scores * scale, 0.0).astype(BF16)
            out = dot(mixed, v_ref[rows, lanes])
            if i % 2:
                out += weight(3) * dot(q, read_ref[i // 2, lanes, :])
            if i >= 2:
                out += weight(4) * dot(q, read_ref[2, lanes, :])
            run_ref[rows, lanes] = out


def far_sum(first, levels, rows, h, q_ref, weight_ref, reads):
    lanes = slice(h * DH, (h + 1) * DH)
    q = q_ref[rows, lanes]
    total = None
    for j, read in enumerate(reads):
        c = h * levels + first + j
        term = weight_ref[rows, c : c + 1] * dot(q, read[lanes, :])
        total = term if total is None else total + term
    return total


def far_kernel(first, levels, run_ref, q_ref, weight_ref, *rest):
    *reads, out_ref = rest
    for i in range(q_ref.shape[0] // BLOCK):
        rows = slice(i * BLOCK, (i + 1) * BLOCK)
        for h in range(out_ref.shape[1] // DH):
            lanes = slice(h * DH, (h + 1) * DH)
            out_ref[rows, lanes] = run_ref[rows, lanes] + far_sum(
                first, levels, rows, h, q_ref, weight_ref, reads
            )


def finish_kernel(first, levels, start, run_ref, q_ref, weight_ref, gain_ref, *rest):
    *reads, out_ref = rest
    for i in range(out_ref.shape[0] // BLOCK):
        rows = slice(start + i * BLOCK, start + (i + 1) * BLOCK)
        for h in range(out_ref.shape[1] // DH):
            lanes = slice(h * DH, (h + 1) * DH)
            total = run_ref[rows, lanes] + far_sum(
                first, levels, rows, h, q_ref, weight_ref, reads
            )
            square = jnp.mean(total * total, -1, keepdims=True)
            scaled = total * lax.rsqrt(square + EPSILON) * gain_ref[:, lanes]
            out_ref[i * BLOCK : (i + 1) * BLOCK, lanes] = scaled.astype(BF16)


def project_kernel(
    chunk,
    info_ref,
    own_ref,
    left_ref,
    right_ref,
    far_left_ref,
    far_right_ref,
    res0_ref,
    res1_ref,
    res2_ref,
    res3_ref,
    w_out_ref,
    gain_ref,
    w_q_ref,
    w_k_ref,
    w_v_ref,
    q_ref,
    k_ref,
    v_ref,
    hidden_ref,
):
    me = info_ref[0]
    group = 4
    width = own_ref.shape[1]

    def rows_of(owner):
        return w_out_ref[pl.ds(pl.multiple_of(owner * width, width), width), :]

    for j in range(own_ref.shape[0] // BLOCK):
        rows = slice(j * BLOCK, (j + 1) * BLOCK)
        block = chunk * (own_ref.shape[0] // BLOCK) + j
        distance = lax.rem(me - block + group, group)
        far_ref = far_left_ref if j == 0 else far_right_ref
        total = dot(own_ref[rows, :], rows_of(me))
        total += dot(left_ref[rows, :], rows_of(lax.rem(me + 3, group)))
        total += dot(right_ref[rows, :], rows_of(lax.rem(me + 1, group)))
        total += dot(far_ref[...], rows_of(lax.rem(me + 2, group)))
        res = jnp.where(
            distance < 2,
            jnp.where(distance == 0, res0_ref[...], res1_ref[...]),
            jnp.where(distance == 2, res2_ref[...], res3_ref[...]),
        )
        hidden = (res.astype(F32) + total).astype(BF16)

        @pl.when(distance == 0)
        def _(hidden=hidden):
            hidden_ref[...] = hidden

        wide = hidden.astype(F32)
        square = jnp.mean(wide * wide, -1, keepdims=True)
        normed = (wide * lax.rsqrt(square + EPSILON) * gain_ref[...]).astype(BF16)
        q_ref[rows, :] = dot(normed, w_q_ref[...]).astype(BF16)
        k_ref[rows, :] = dot(normed, w_k_ref[...]).astype(BF16)
        v_ref[rows, :] = dot(normed, w_v_ref[...]).astype(BF16)


def attend_kernel(halo, info_ref, q_ref, k_ref, v_ref, k_before_ref, v_before_ref, out_ref):
    scale = DH ** (-0.5)
    t = lax.broadcasted_iota(jnp.int32, (BLOCK, 2 * BLOCK), 0) + BLOCK
    s = lax.broadcasted_iota(jnp.int32, (BLOCK, 2 * BLOCK), 1)
    distance = t - s
    for h in range(out_ref.shape[1] // DH):
        lanes = slice(h * DH, (h + 1) * DH)
        window = info_ref[1 + h]
        allowed = (distance >= 0) & (distance < window)
        for i in range(out_ref.shape[0] // BLOCK):
            rows = slice(i * BLOCK, (i + 1) * BLOCK)
            if i == 0:
                k_before = k_before_ref[-BLOCK:, lanes]
                v_before = v_before_ref[-BLOCK:, lanes]
            else:
                k_before = k_ref[(i - 1) * BLOCK : i * BLOCK, lanes]
                v_before = v_ref[(i - 1) * BLOCK : i * BLOCK, lanes]
            k = jnp.concatenate([k_before, k_ref[rows, lanes]], 0)
            v = jnp.concatenate([v_before, v_ref[rows, lanes]], 0)
            valid = allowed
            if halo and i == 0:
                valid = allowed & ((s >= BLOCK) | (info_ref[3] > 0))
            scores = dot(q_ref[rows, lanes], k, ((1,), (1,))) * scale
            scores = jnp.where(valid, scores, -1e30)
            weights = jnp.exp(scores - jnp.max(scores, -1, keepdims=True))
            total = jnp.sum(weights, -1, keepdims=True)
            probs = (weights / total).astype(BF16)
            out_ref[rows, lanes] = dot(probs, v).astype(BF16)


def shift(array, axis, route):
    size = lax.axis_size(axis)
    pairs = [(i, route(i)) for i in range(size) if 0 <= route(i) < size]
    return lax.ppermute(array, axis, pairs)


def per_device(
    queries,
    keys,
    values,
    level_index,
    level_table,
    head_gain,
    residual,
    w_out,
    norm_gain,
    w_qkv,
    windows,
):
    tokens, width = queries.shape
    heads = width // DH
    levels = level_table.shape[2]
    group = lax.axis_size("head")
    model = residual.shape[1]
    head = lax.axis_index("head")
    position = lax.axis_index("ctx")
    info = jnp.concatenate(
        [
            head[None],
            lax.dynamic_slice_in_dim(windows, head * heads, heads),
            position[None],
        ]
    ).astype(jnp.int32)
    rates = jnp.array(
        [STRETCH ** (-0.5)] + [(STRETCH * 2**b) ** (-0.5) for b in range(levels - 1)], F32
    )
    table = (level_table * rates).reshape(level_table.shape[0], heads * levels)
    table = jnp.pad(table, ((0, 0), (0, DH - heads * levels)))
    gain = head_gain.reshape(1, width)

    state, send, near = call(
        state_kernel,
        [((width, DH), F32), ((width, DH), BF16), ((3, width, DH), BF16)],
        (keys, values),
        [VMEM] * 2,
        2 * tokens * width * DH,
        2**20,
        "state",
    )
    (weight,) = call(
        weight_kernel,
        [((tokens, DH), F32)],
        (level_index.reshape(1, tokens), table),
        [VMEM] * 2,
        2 * tokens * DH * DH,
        2**20,
        "weight",
    )
    (run,) = call(
        lambda *refs: local_kernel(levels, *refs),
        [((tokens, width), F32)],
        (queries, keys, values, near, weight),
        [VMEM] * 5,
        2 * tokens * width * 1024,
        2**22,
        "local",
    )

    reads = []
    for b, route in enumerate(CTX_ROUTES):
        other = shift(send, "ctx", lambda i, r=route: i ^ r)
        bit = (position >> b) & 1
        reads.append(other * bit.astype(BF16))
        state = state + other.astype(F32)
        send = state.astype(BF16)

    res = [residual] + [
        shift(residual, "head", lambda i, d=d: (i + d) % group) for d in range(1, group)
    ]
    local_levels = levels - len(reads)
    early = len(reads) - 2
    (run,) = call(
        lambda *refs: far_kernel(local_levels, levels, *refs),
        [((tokens, width), F32)],
        (run, queries, weight, *reads[:early]),
        [VMEM] * (3 + early),
        2 * tokens * width * DH * early,
        2**22,
        "far",
    )
    chunk_rows = tokens // 2
    gathered = {}
    for chunk in (1, 0):
        (own,) = call(
            lambda *refs, c=chunk: finish_kernel(
                local_levels + early, levels, c * chunk_rows, *refs
            ),
            [((chunk_rows, width), BF16)],
            (run, queries, weight, gain, *reads[early:]),
            [VMEM] * (4 + len(reads) - early),
            2 * chunk_rows * width * DH * 2,
            2**20,
            "finish",
        )
        half = chunk_rows // 2
        left = shift(own, "head", lambda i: (i + 1) % group)
        right = shift(own, "head", lambda i: (i - 1) % group)
        far_left = shift(left[:half], "head", lambda i: (i + 1) % group)
        far_right = shift(right[half:], "head", lambda i: (i - 1) % group)
        gathered[chunk] = (own, left, right, far_left, far_right)
    w_parts = [
        lax.dynamic_slice(w_qkv, (0, part * model + head * width), (model, width))
        for part in range(3)
    ]
    out = {}
    for chunk in (1, 0):
        out[chunk] = call(
            lambda *refs, c=chunk: project_kernel(c, *refs),
            [((chunk_rows, width), BF16)] * 3 + [((BLOCK, model), BF16)],
            (info, *gathered[chunk], *res, w_out, norm_gain.reshape(1, model), *w_parts),
            [SMEM] + [VMEM] * 14,
            2 * chunk_rows * model * (model + 3 * width),
            2**23,
            "project",
            vmem=32,
        )
    hidden = jnp.where(head >= 2, out[1][3], out[0][3])
    tail = jnp.concatenate([out[1][1][-BLOCK:], out[1][2][-BLOCK:]], 1)
    before = shift(tail, "ctx", lambda i: i + 1)
    attended = []
    for chunk in (0, 1):
        q, k, v, _ = out[chunk]
        if chunk:
            k_before, v_before = out[0][1], out[0][2]
        else:
            k_before, v_before = before[:, :width], before[:, width:]
        (block,) = call(
            lambda *refs, c=chunk: attend_kernel(c == 0, *refs),
            [((chunk_rows, width), BF16)],
            (info, q, k, v, k_before, v_before),
            [SMEM] + [VMEM] * 5,
            4 * chunk_rows * 512 * width,
            2**20,
            "attend",
        )
        attended.append(block)
    return hidden, jnp.concatenate(attended, 0)


def solution(mesh):
    in_specs = (
        P("ctx", "head"),
        P("ctx", "head"),
        P("ctx", "head"),
        P("ctx"),
        P(None, "head", None),
        P("head"),
        P(("ctx", "head"), None),
        P(),
        P(),
        P(),
        P(),
    )
    out_specs = (P(("ctx", "head"), None), P("ctx", "head"))
    return jax.shard_map(
        per_device, mesh=mesh, in_specs=in_specs, out_specs=out_specs, check_vma=False
    )
```

time: 232 us -> 103 us (0.44); the launches traced: 229 us -> 102 us
  matrix products: 51.3 us -> 0 us
  local copies, waits for them, and re-layouts: 53.2 us -> 10 us
  starting transfers between devices: 7.34 us -> 47.1 us
  blocking collectives: 34.4 us -> 0 us
  waiting for transfers between devices: 53.8 us -> 21.8 us
  Pallas kernels: 0 us -> 19.6 us
  between operations: 14.4 us -> 0.97 us
  other arithmetic: 12.9 us -> 2.74 us
    all_gather x1 -> x0, waiting for transfers between devices: 53 us -> none  [per_device(): piece = lax.all_gather(device_state[None], 'ctx', axis=0, tiled=True)]
    dot_general x13 -> x0, matrix products: 45.2 us -> none  [the longest x1 10.7 us: per_device(): remote = jnp.einsum('nb,nxy->bxy', member, piece, precision=PRECISE)]
    ppermute x1 -> x18, starting transfers between devices: 7.3 us -> 47.1 us  [shift(): return lax.ppermute(array, axis, pairs)]
    all_to_all x2 -> x0, blocking collectives: 34.4 us -> none  [the longest x1 21.6 us: per_device(): lax.all_to_all(split_qkv, 'head', split_axis=2, concat_axis=0, tiled=True)]
    ppermute x1 -> x18, waiting for transfers between devices: 0.8 us -> 21.8 us  [shift(): return lax.ppermute(array, axis, pairs)]
    pallas_call x0 -> x10, Pallas kernels: none -> 19.6 us  [call(): pl.pallas_call(kernel, out_shape=[jax.ShapeDtypeStruct(s, d) for s, d in...]
    reshape x10 -> x1, local copies, waits for them, and re-layouts: 15.1 us -> 0.08 us  [per_device(): table = (level_table * rates).reshape(level_table.shape[0], heads * levels)]
    slice x9 -> x7, local copies, waits for them, and re-layouts: 8.5 us -> 0.73 us  [the longest x2 0.67 us: per_device(): far_right = shift(right[half:], 'head', lambda i: (i - 1) % group)]
  transfers between devices with their start and end apart: 2 -> 18, of which waited for: 2 -> 9; matrix products, arithmetic and copies ran while one was open for 13% -> 4% of each run, Pallas kernels for 0% -> 16%
where the time goes in v1:
time: 103 us; the launch traced here: 102 us
  starting transfers between devices  47.1 us (46%)
  waiting for transfers between devices  21.8 us (21%)
  Pallas kernels  19.6 us (19%)
  local copies, waits for them, and re-layouts  10 us (10%)
  other arithmetic  2.74 us (3%)
    ppermute x18, starting transfers between devices, shift(): return lax.ppermute(array, axis, pairs)  47.1 us
    ppermute x18, waiting for transfers between devices, shift(): return lax.ppermute(array, axis, pairs)  21.8 us
    pallas_call x10, Pallas kernels, call(): pl.pallas_call(kernel, out_shape=[jax.ShapeDtypeStruct(s, d) for s, d in...  19.6 us
    unnamed x24, local copies, waits for them, and re-layouts  7.56 us
  transfers between devices with their start and end apart: 18, of which 9 were waited for; matrix products, arithmetic and copies ran while one was open for 4% of the time, Pallas kernels for 16%

profile of v1, /device:TPU:7, one launch (start us, length us, event | category | flops | bytes accessed | tf_op | source)
XLA Modules:
  0.0 102.2 jit_solution(17196460379075797710)
XLA Ops:
  0.7 1.1 %copy-done.2 = bf16[1024,256]{1,0:T(8,128)(2,1)S(1)} copy-done((bf16[1024,256]{1,0:T(8,128)(2,1)S(1)}, bf16[1024,256]{1,0:T(8,128)(2,1)}, u32[]{:S(2)}) %copy-start.2) | copy-done | bytes 524312
  1.7 1.0 %copy-done.4 = bf16[1024,256]{1,0:T(8,128)(2,1)S(1)} copy-done((bf16[1024,256]{1,0:T(8,128)(2,1)S(1)}, bf16[1024,256]{1,0:T(8,128)(2,1)}, u32[]{:S(2)}) %copy-start.4) | copy-done | bytes 524312
  5.9 1.0 %copy-done = bf16[1024,256]{1,0:T(8,128)(2,1)S(1)} copy-done((bf16[1024,256]{1,0:T(8,128)(2,1)S(1)}, bf16[1024,256]{1,0:T(8,128)(2,1)}, u32[]{:S(2)}) %copy-start) | copy-done | bytes 524312
  6.9 1.0 %copy-done.3 = bf16[1024,256]{1,0:T(8,128)(2,1)S(1)} copy-done((bf16[1024,256]{1,0:T(8,128)(2,1)S(1)}, bf16[1024,256]{1,0:T(8,128)(2,1)}, u32[]{:S(2)}) %copy-start.3) | copy-done | bytes 524312
  8.0 1.0 %copy-done.5 = bf16[1024,256]{1,0:T(8,128)(2,1)S(1)} copy-done((bf16[1024,256]{1,0:T(8,128)(2,1)S(1)}, bf16[1024,256]{1,0:T(8,128)(2,1)}, u32[]{:S(2)}) %copy-start.5) | copy-done | bytes 524312
  9.0 1.4 %local.1.refs_0_ = f32[1024,256]{1,0:T(8,128)S(1)} custom-call(bf16[1024,256]{1,0:T(8,128)(2,1)S(1)} %copy-done, bf16[1024,256]{1,0:T(8,128)(2,1)S(1)} %copy-done.3, bf16[1024,256]{1,0:T(8,128)(2,1)S(1)} %copy-done.5, bf16[3,256,128]{2,1,0:T(8,128)(2,1)S(1)} %get-tuple-element.13.refs_3_, f32[1024,128]{1,0:T(8,128)S(1)} %weight.1.refs_4_.refs_2_), custom_call_target="tpu_custom_call" | custom-call | flops 536870912 | bytes 4194304 | tf_op jit(solution)/shard_map/local/pallas_call | solution.py:26
  11.0 3.1 %collective-permute-done.1 = bf16[256,128]{1,0:T(8,128)(2,1)S(1)} collective-permute-done((bf16[256,128]{1,0:T(8,128)(2,1)S(1)}, bf16[256,128]{1,0:T(8,128)(2,1)S(1)}, u32[]{:S(2)}, u32[]{:S(2)}) %collective-permute-start.1) | collective-permute-done | bytes 65568 | tf_op jit(solution)/shard_map/ppermute | solution.py:221
  14.1 2.0 %collective-permute-start.2 = (bf16[256,128]{1,0:T(8,128)(2,1)S(1)}, bf16[256,128]{1,0:T(8,128)(2,1)S(1)}, u32[]{:S(2)}, u32[]{:S(2)}) collective-permute-start(bf16[256,128]{1,0:T(8,128)(2,1)S(1)} %get-tuple-element.24), channel_id=1, source_target_pairs={{0,24},{4,28},{8,16},{12,20},{16,8},{20,12},{24,0},{28,4},{32,56},... | collective-permute-start | bytes 196616 | tf_op jit(solution)/shard_map/ppermute | solution.py:221
  16.1 2.4 %collective-permute-done.2 = bf16[256,128]{1,0:T(8,128)(2,1)S(1)} collective-permute-done((bf16[256,128]{1,0:T(8,128)(2,1)S(1)}, bf16[256,128]{1,0:T(8,128)(2,1)S(1)}, u32[]{:S(2)}, u32[]{:S(2)}) %collective-permute-start.2) | collective-permute-done | bytes 65568 | tf_op jit(solution)/shard_map/ppermute | solution.py:221
  18.6 1.7 %collective-permute-start.3 = (bf16[256,128]{1,0:T(8,128)(2,1)S(1)}, bf16[256,128]{1,0:T(8,128)(2,1)S(1)}, u32[]{:S(2)}, u32[]{:S(2)}) collective-permute-start(bf16[256,128]{1,0:T(8,128)(2,1)S(1)} %fusion.1), channel_id=1, source_target_pairs={{0,32},{4,36},{8,40},{12,44},{16,48},{20,52},{24,56},{28,60},{32,0... | collective-permute-start | bytes 196616 | tf_op jit(solution)/shard_map/ppermute | solution.py:221
  20.3 1.6 %collective-permute-done.3 = bf16[256,128]{1,0:T(8,128)(2,1)S(1)} collective-permute-done((bf16[256,128]{1,0:T(8,128)(2,1)S(1)}, bf16[256,128]{1,0:T(8,128)(2,1)S(1)}, u32[]{:S(2)}, u32[]{:S(2)}) %collective-permute-start.3) | collective-permute-done | bytes 65568 | tf_op jit(solution)/shard_map/ppermute | solution.py:221
  22.0 3.1 %collective-permute-start.4 = (bf16[256,128]{1,0:T(8,128)(2,1)S(1)}, bf16[256,128]{1,0:T(8,128)(2,1)S(1)}, u32[]{:S(2)}, u32[]{:S(2)}) collective-permute-start(bf16[256,128]{1,0:T(8,128)(2,1)S(1)} %fusion.2), channel_id=1, source_target_pairs={{0,64},{4,68},{8,72},{12,76},{16,80},{20,84},{24,88},{28,92},{32,9... | collective-permute-start | bytes 196616 | tf_op jit(solution)/shard_map/ppermute | solution.py:221
  25.1 1.3 %far.1.refs_0_ = f32[1024,256]{1,0:T(8,128)S(1)} custom-call(f32[1024,256]{1,0:T(8,128)S(1)} %local.1.refs_0_, bf16[1024,256]{1,0:T(8,128)(2,1)S(1)} %copy-done.1, f32[1024,128]{1,0:T(8,128)S(1)} %weight.1.refs_4_.refs_2_, bf16[256,128]{1,0:T(8,128)(2,1)S(1)} %broadcast_multiply_fusion.5.refs_3_, bf16[256,128]{1,0:T(8,128)(2,1)S(1)} %broadcast_multiply_fusion.4.refs_4_, ...), custom_call_target="tpu_custom_call" | custom-call | flops 268435456 | bytes 4194304 | tf_op jit(solution)/shard_map/far/pallas_call | solution.py:26
  26.8 5.4 %collective-permute-start.5 = (bf16[256,128]{1,0:T(8,128)(2,1)S(1)}, bf16[256,128]{1,0:T(8,128)(2,1)S(1)}, u32[]{:S(2)}, u32[]{:S(2)}) collective-permute-start(bf16[256,128]{1,0:T(8,128)(2,1)S(1)} %add_convert_fusion), channel_id=1, source_target_pairs={{0,192},{4,196},{8,200},{12,204},{16,208},{20,212},{24,216},{28,22... | collective-permute-start | bytes 196616 | tf_op jit(solution)/shard_map/ppermute | solution.py:221
  32.2 1.7 %collective-permute-done.5 = bf16[256,128]{1,0:T(8,128)(2,1)S(1)} collective-permute-done((bf16[256,128]{1,0:T(8,128)(2,1)S(1)}, bf16[256,128]{1,0:T(8,128)(2,1)S(1)}, u32[]{:S(2)}, u32[]{:S(2)}) %collective-permute-start.5) | collective-permute-done | bytes 65568 | tf_op jit(solution)/shard_map/ppermute | solution.py:221
  34.6 2.8 %collective-permute-start.7 = (bf16[512,256]{1,0:T(8,128)(2,1)S(1)}, bf16[512,256]{1,0:T(8,128)(2,1)S(1)}, u32[]{:S(2)}, u32[]{:S(2)}) collective-permute-start(bf16[512,256]{1,0:T(8,128)(2,1)S(1)} %finish.2.refs_1_), channel_id=1, source_target_pairs={{0,3},{1,0},{2,1},{3,2},{4,7},{5,4},{6,5},{7,6},{8,11},{9,8},{10,9... | collective-permute-start | bytes 786440 | tf_op jit(solution)/shard_map/ppermute | solution.py:221
  38.1 2.7 %collective-permute-start.14 = (bf16[512,256]{1,0:T(8,128)(2,1)S(1)}, bf16[512,256]{1,0:T(8,128)(2,1)S(1)}, u32[]{:S(2)}, u32[]{:S(2)}) collective-permute-start(bf16[512,256]{1,0:T(8,128)(2,1)S(1)} %finish.3.refs_1_), channel_id=1, source_target_pairs={{0,3},{1,0},{2,1},{3,2},{4,7},{5,4},{6,5},{7,6},{8,11},{9,8},{10,9... | collective-permute-start | bytes 786440 | tf_op jit(solution)/shard_map/ppermute | solution.py:221
  40.9 2.7 %collective-permute-start.12 = (bf16[256,1024]{1,0:T(8,128)(2,1)}, bf16[256,1024]{1,0:T(8,128)(2,1)}, u32[]{:S(2)}, u32[]{:S(2)}) collective-permute-start(bf16[256,1024]{1,0:T(8,128)(2,1)} %refs_6_.3), channel_id=1, source_target_pairs={{0,3},{1,0},{2,1},{3,2},{4,7},{5,4},{6,5},{7,6},{8,11},{9,8},{10,9... | collective-permute-start | bytes 1572872 | tf_op jit(solution)/shard_map/ppermute | solution.py:221
  45.1 3.1 %collective-permute-start.9 = (bf16[256,256]{1,0:T(8,128)(2,1)}, bf16[256,256]{1,0:T(8,128)(2,1)S(1)}, u32[]{:S(2)}, u32[]{:S(2)}) collective-permute-start(bf16[256,256]{1,0:T(8,128)(2,1)} %slice.33), channel_id=1, source_target_pairs={{0,3},{1,0},{2,1},{3,2},{4,7},{5,4},{6,5},{7,6},{8,11},{9,8},{10,9... | collective-permute-start | bytes 393224 | tf_op jit(solution)/shard_map/ppermute | solution.py:221
  48.2 1.5 %constant_dynamic-slice_fusion = (bf16[1024,256]{1,0:T(8,128)(2,1)S(1)}, bf16[1024,256]{1,0:T(8,128)(2,1)S(1)}, bf16[1024,256]{1,0:T(8,128)(2,1)S(1)}) fusion(bf16[1024,3072]{1,0:T(8,128)(2,1)} %param.21, s32[]{:T(128)S(6)} %select_n.24, s32[]{:T(128)S(6)} %select_n.22, s32[]{:T(128)S(6)} %select_n.23), kind=kLoop, calls=%fused_computation.18 | loop fusion | bytes 3145740 | tf_op jit(solution)/shard_map/dynamic_slice | solution.py:329
  49.9 7.2 %collective-permute-done.12.refs_9_ = bf16[256,1024]{1,0:T(8,128)(2,1)} collective-permute-done((bf16[256,1024]{1,0:T(8,128)(2,1)}, bf16[256,1024]{1,0:T(8,128)(2,1)}, u32[]{:S(2)}, u32[]{:S(2)}) %collective-permute-start.12) | collective-permute-done | bytes 524320 | tf_op jit(solution)/shard_map/ppermute | solution.py:221
  57.1 3.9 %collective-permute-start.16 = (bf16[256,256]{1,0:T(8,128)(2,1)S(1)}, bf16[256,256]{1,0:T(8,128)(2,1)S(1)}, u32[]{:S(2)}, u32[]{:S(2)}) collective-permute-start(bf16[256,256]{1,0:T(8,128)(2,1)S(1)} %slice.35), channel_id=1, source_target_pairs={{0,3},{1,0},{2,1},{3,2},{4,7},{5,4},{6,5},{7,6},{8,11},{9,8},{10,9... | collective-permute-start | bytes 393224 | tf_op jit(solution)/shard_map/ppermute | solution.py:221
  61.0 7.3 %collective-permute-start.15 = (bf16[256,256]{1,0:T(8,128)(2,1)S(1)}, bf16[256,256]{1,0:T(8,128)(2,1)S(1)}, u32[]{:S(2)}, u32[]{:S(2)}) collective-permute-start(bf16[256,256]{1,0:T(8,128)(2,1)S(1)} %slice.34), channel_id=1, source_target_pairs={{0,1},{1,2},{2,3},{3,0},{4,5},{5,6},{6,7},{7,4},{8,9},{9,10},{10,1... | collective-permute-start | bytes 393224 | tf_op jit(solution)/shard_map/ppermute | solution.py:221
  68.2 2.3 %collective-permute-done.10.refs_7_ = bf16[256,1024]{1,0:T(8,128)(2,1)} collective-permute-done((bf16[256,1024]{1,0:T(8,128)(2,1)}, bf16[256,1024]{1,0:T(8,128)(2,1)}, u32[]{:S(2)}, u32[]{:S(2)}) %collective-permute-start.10) | collective-permute-done | bytes 524320 | tf_op jit(solution)/shard_map/ppermute | solution.py:221
  70.5 2.8 %collective-permute-done.8.refs_4_ = bf16[256,256]{1,0:T(8,128)(2,1)S(1)} collective-permute-done((bf16[256,256]{1,0:T(8,128)(2,1)S(1)}, bf16[256,256]{1,0:T(8,128)(2,1)S(1)}, u32[]{:S(2)}, u32[]{:S(2)}) %collective-permute-start.8) | collective-permute-done | bytes 131104 | tf_op jit(solution)/shard_map/ppermute | solution.py:221
  73.4 1.6 %copy-done.8 = bf16[1024,1024]{1,0:T(8,128)(2,1)S(1)} copy-done((bf16[1024,1024]{1,0:T(8,128)(2,1)S(1)}, bf16[1024,1024]{1,0:T(8,128)(2,1)}, u32[]{:S(2)}) %copy-start.8) | copy-done | bytes 2097176
  75.0 5.1 %project.2 = (bf16[512,256]{1,0:T(8,128)(2,1)S(1)}, bf16[512,256]{1,0:T(8,128)(2,1)S(1)}, bf16[512,256]{1,0:T(8,128)(2,1)S(1)}, bf16[256,1024]{1,0:T(8,128)(2,1)S(1)}) custom-call(s32[4]{0:T(128)S(1)} %pad_add_fusion.refs_0_, bf16[512,256]{1,0:T(8,128)(2,1)S(1)} %finish.2.refs_1_, bf16[512,256]{1,0:T(8,128)(2,1)S(1)} %collective-permute-done.6.refs_2_, ...), custom_call_target="tpu_custom_call" | custom-call | flops 1879048192 | bytes 8388608 | tf_op jit(solution)/shard_map/project/pallas_call | solution.py:26
  80.2 10.5 %collective-permute-start.17 = (bf16[256,512]{1,0:T(8,128)(2,1)S(1)}, bf16[256,512]{1,0:T(8,128)(2,1)S(1)}, u32[]{:S(2)}, u32[]{:S(2)}) collective-permute-start(bf16[256,512]{1,0:T(8,128)(2,1)S(1)} %pad_maximum_fusion.1), channel_id=1, source_target_pairs={{0,4},{4,8},{8,12},{12,16},{16,20},{20,24},{24,28},{28,32},{32,36}... | collective-permute-start | bytes 786440 | tf_op jit(solution)/shard_map/ppermute | solution.py:221
  90.6 5.0 %project.3 = (bf16[512,256]{1,0:T(8,128)(2,1)S(1)}, bf16[512,256]{1,0:T(8,128)(2,1)S(1)}, bf16[512,256]{1,0:T(8,128)(2,1)S(1)}, bf16[256,1024]{1,0:T(8,128)(2,1)S(1)}) custom-call(s32[4]{0:T(128)S(1)} %pad_add_fusion.refs_0_, bf16[512,256]{1,0:T(8,128)(2,1)S(1)} %finish.3.refs_1_, bf16[512,256]{1,0:T(8,128)(2,1)S(1)} %collective-permute-done.13.refs_2_, ...), custom_call_target="tpu_custom_call" | custom-call | flops 1879048192 | bytes 8388608 | tf_op jit(solution)/shard_map/project/pallas_call | solution.py:26
  95.7 2.4 %attend.3 = bf16[512,256]{1,0:T(8,128)(2,1)S(1)} custom-call(s32[4]{0:T(128)S(1)} %pad_add_fusion.refs_0_, bf16[512,256]{1,0:T(8,128)(2,1)S(1)} %get-tuple-element.23.refs_1_, bf16[512,256]{1,0:T(8,128)(2,1)S(1)} %get-tuple-element.21.refs_2_, bf16[512,256]{1,0:T(8,128)(2,1)S(1)} %get-tuple-element.22.refs_3_, ...), custom_call_target="tpu_custom_call" | custom-call | flops 268435456 | bytes 1048576 | tf_op jit(solution)/shard_map/attend/pallas_call | solution.py:26
  98.1 0.9 broadcast_select_fusion
  99.0 2.4 %attend.2 = bf16[512,256]{1,0:T(8,128)(2,1)S(1)} custom-call(s32[4]{0:T(128)S(1)} %pad_add_fusion.refs_0_, bf16[512,256]{1,0:T(8,128)(2,1)S(1)} %get-tuple-element.18.refs_1_, bf16[512,256]{1,0:T(8,128)(2,1)S(1)} %get-tuple-element.19.refs_2_.refs_4_, bf16[512,256]{1,0:T(8,128)(2,1)S(1)} %get-tuple-element.20.refs_3_.refs_5_, ...), custom_call_target="tpu_custom_call" | custom-call | flops 268435456 | bytes 1048576 | tf_op jit(solution)/shard_map/attend/pallas_call | solution.py:26
  (66 shorter events, 8.3 us)
Async XLA Ops:
  0.6 24.4 %copy-start.1 = (bf16[1024,256]{1,0:T(8,128)(2,1)S(1)}, bf16[1024,256]{1,0:T(8,128)(2,1)}, u32[]{:S(2)}) copy-start(bf16[1024,256]{1,0:T(8,128)(2,1)} %refs_1_.7) | copy-start | bytes 1572868
  0.6 1.1 %copy-start.2 = (bf16[1024,256]{1,0:T(8,128)(2,1)S(1)}, bf16[1024,256]{1,0:T(8,128)(2,1)}, u32[]{:S(2)}) copy-start(bf16[1024,256]{1,0:T(8,128)(2,1)} %refs_1_.4) | copy-start | bytes 1572868
  1.7 1.0 %copy-start.4 = (bf16[1024,256]{1,0:T(8,128)(2,1)S(1)}, bf16[1024,256]{1,0:T(8,128)(2,1)}, u32[]{:S(2)}) copy-start(bf16[1024,256]{1,0:T(8,128)(2,1)} %refs_2_.1) | copy-start | bytes 1572868
  2.8 31.1 %copy-start.7 = (f32[256]{0:T(256)S(1)}, f32[256]{0:T(256)}, u32[]{:S(2)}) copy-start(f32[256]{0:T(256)} %param.17) | copy-start | bytes 3076
  3.1 7.2 %collective-permute-start = (bf16[256,128]{1,0:T(8,128)(2,1)S(1)}, bf16[256,128]{1,0:T(8,128)(2,1)S(1)}, u32[]{:S(2)}, u32[]{:S(2)}) collective-permute-start(bf16[256,128]{1,0:T(8,128)(2,1)S(1)} %get-tuple-element.14), channel_id=1, source_target_pairs={{0,4},{4,0},{8,12},{12,8},{16,20},{20,16},{24,28},{28,24},{32,36},... | collective-permute-start | bytes 196616 | tf_op jit(solution)/shard_map/ppermute | solution.py:221
  4.9 0.7 copy-start.6
  5.9 1.0 %copy-start = (bf16[1024,256]{1,0:T(8,128)(2,1)S(1)}, bf16[1024,256]{1,0:T(8,128)(2,1)}, u32[]{:S(2)}) copy-start(bf16[1024,256]{1,0:T(8,128)(2,1)} %refs_1_.7) | copy-start | bytes 1572868
  6.9 1.0 %copy-start.3 = (bf16[1024,256]{1,0:T(8,128)(2,1)S(1)}, bf16[1024,256]{1,0:T(8,128)(2,1)}, u32[]{:S(2)}) copy-start(bf16[1024,256]{1,0:T(8,128)(2,1)} %refs_1_.4) | copy-start | bytes 1572868
  8.0 1.0 %copy-start.5 = (bf16[1024,256]{1,0:T(8,128)(2,1)S(1)}, bf16[1024,256]{1,0:T(8,128)(2,1)}, u32[]{:S(2)}) copy-start(bf16[1024,256]{1,0:T(8,128)(2,1)} %refs_2_.1) | copy-start | bytes 1572868
  10.4 3.7 %collective-permute-start.1 = (bf16[256,128]{1,0:T(8,128)(2,1)S(1)}, bf16[256,128]{1,0:T(8,128)(2,1)S(1)}, u32[]{:S(2)}, u32[]{:S(2)}) collective-permute-start(bf16[256,128]{1,0:T(8,128)(2,1)S(1)} %fusion), channel_id=1, source_target_pairs={{0,8},{4,12},{8,0},{12,4},{16,24},{20,28},{24,16},{28,20},{32,40},... | collective-permute-start | bytes 196616 | tf_op jit(solution)/shard_map/ppermute | solution.py:221
  14.1 4.4 %collective-permute-start.2 = (bf16[256,128]{1,0:T(8,128)(2,1)S(1)}, bf16[256,128]{1,0:T(8,128)(2,1)S(1)}, u32[]{:S(2)}, u32[]{:S(2)}) collective-permute-start(bf16[256,128]{1,0:T(8,128)(2,1)S(1)} %get-tuple-element.24), channel_id=1, source_target_pairs={{0,24},{4,28},{8,16},{12,20},{16,8},{20,12},{24,0},{28,4},{32,56},... | collective-permute-start | bytes 196616 | tf_op jit(solution)/shard_map/ppermute | solution.py:221
  18.6 3.4 %collective-permute-start.3 = (bf16[256,128]{1,0:T(8,128)(2,1)S(1)}, bf16[256,128]{1,0:T(8,128)(2,1)S(1)}, u32[]{:S(2)}, u32[]{:S(2)}) collective-permute-start(bf16[256,128]{1,0:T(8,128)(2,1)S(1)} %fusion.1), channel_id=1, source_target_pairs={{0,32},{4,36},{8,40},{12,44},{16,48},{20,52},{24,56},{28,60},{32,0... | collective-permute-start | bytes 196616 | tf_op jit(solution)/shard_map/ppermute | solution.py:221
  22.0 4.7 %collective-permute-start.4 = (bf16[256,128]{1,0:T(8,128)(2,1)S(1)}, bf16[256,128]{1,0:T(8,128)(2,1)S(1)}, u32[]{:S(2)}, u32[]{:S(2)}) collective-permute-start(bf16[256,128]{1,0:T(8,128)(2,1)S(1)} %fusion.2), channel_id=1, source_target_pairs={{0,64},{4,68},{8,72},{12,76},{16,80},{20,84},{24,88},{28,92},{32,9... | collective-permute-start | bytes 196616 | tf_op jit(solution)/shard_map/ppermute | solution.py:221
  25.1 24.6 %copy-start.11 = (s32[8]{0:T(128)S(1)}, s32[8]{0:T(128)}, u32[]{:S(2)}) copy-start(s32[8]{0:T(128)} %param.22) | copy-start | bytes 100
  25.1 48.3 %copy-start.10 = (f32[1024]{0:T(1024)S(1)}, f32[1024]{0:T(1024)}, u32[]{:S(2)}) copy-start(f32[1024]{0:T(1024)} %param.20) | copy-start | bytes 12292
  26.8 7.1 %collective-permute-start.5 = (bf16[256,128]{1,0:T(8,128)(2,1)S(1)}, bf16[256,128]{1,0:T(8,128)(2,1)S(1)}, u32[]{:S(2)}, u32[]{:S(2)}) collective-permute-start(bf16[256,128]{1,0:T(8,128)(2,1)S(1)} %add_convert_fusion), channel_id=1, source_target_pairs={{0,192},{4,196},{8,200},{12,204},{16,208},{20,212},{24,216},{28,22... | collective-permute-start | bytes 196616 | tf_op jit(solution)/shard_map/ppermute | solution.py:221
  34.6 8.9 %collective-permute-start.7 = (bf16[512,256]{1,0:T(8,128)(2,1)S(1)}, bf16[512,256]{1,0:T(8,128)(2,1)S(1)}, u32[]{:S(2)}, u32[]{:S(2)}) collective-permute-start(bf16[512,256]{1,0:T(8,128)(2,1)S(1)} %finish.2.refs_1_), channel_id=1, source_target_pairs={{0,3},{1,0},{2,1},{3,2},{4,7},{5,4},{6,5},{7,6},{8,11},{9,8},{10,9... | collective-permute-start | bytes 786440 | tf_op jit(solution)/shard_map/ppermute | solution.py:221
  37.4 6.4 %collective-permute-start.6 = (bf16[512,256]{1,0:T(8,128)(2,1)S(1)}, bf16[512,256]{1,0:T(8,128)(2,1)S(1)}, u32[]{:S(2)}, u32[]{:S(2)}) collective-permute-start(bf16[512,256]{1,0:T(8,128)(2,1)S(1)} %finish.2.refs_1_), channel_id=1, source_target_pairs={{0,1},{1,2},{2,3},{3,0},{4,5},{5,6},{6,7},{7,4},{8,9},{9,10},{10,1... | collective-permute-start | bytes 786440 | tf_op jit(solution)/shard_map/ppermute | solution.py:221
  38.1 7.0 %collective-permute-start.14 = (bf16[512,256]{1,0:T(8,128)(2,1)S(1)}, bf16[512,256]{1,0:T(8,128)(2,1)S(1)}, u32[]{:S(2)}, u32[]{:S(2)}) collective-permute-start(bf16[512,256]{1,0:T(8,128)(2,1)S(1)} %finish.3.refs_1_), channel_id=1, source_target_pairs={{0,3},{1,0},{2,1},{3,2},{4,7},{5,4},{6,5},{7,6},{8,11},{9,8},{10,9... | collective-permute-start | bytes 786440 | tf_op jit(solution)/shard_map/ppermute | solution.py:221
  40.9 7.3 %collective-permute-start.13 = (bf16[512,256]{1,0:T(8,128)(2,1)S(1)}, bf16[512,256]{1,0:T(8,128)(2,1)S(1)}, u32[]{:S(2)}, u32[]{:S(2)}) collective-permute-start(bf16[512,256]{1,0:T(8,128)(2,1)S(1)} %finish.3.refs_1_), channel_id=1, source_target_pairs={{0,1},{1,2},{2,3},{3,0},{4,5},{5,6},{6,7},{7,4},{8,9},{9,10},{10,1... | collective-permute-start | bytes 786440 | tf_op jit(solution)/shard_map/ppermute | solution.py:221
  40.9 16.2 %collective-permute-start.12 = (bf16[256,1024]{1,0:T(8,128)(2,1)}, bf16[256,1024]{1,0:T(8,128)(2,1)}, u32[]{:S(2)}, u32[]{:S(2)}) collective-permute-start(bf16[256,1024]{1,0:T(8,128)(2,1)} %refs_6_.3), channel_id=1, source_target_pairs={{0,3},{1,0},{2,1},{3,2},{4,7},{5,4},{6,5},{7,6},{8,11},{9,8},{10,9... | collective-permute-start | bytes 1572872 | tf_op jit(solution)/shard_map/ppermute | solution.py:221
  43.5 17.4 %collective-permute-start.11 = (bf16[256,1024]{1,0:T(8,128)(2,1)}, bf16[256,1024]{1,0:T(8,128)(2,1)}, u32[]{:S(2)}, u32[]{:S(2)}) collective-permute-start(bf16[256,1024]{1,0:T(8,128)(2,1)} %refs_6_.3), channel_id=1, source_target_pairs={{0,2},{1,3},{2,0},{3,1},{4,6},{5,7},{6,4},{7,5},{8,10},{9,11},{10,... | collective-permute-start | bytes 1572872 | tf_op jit(solution)/shard_map/ppermute | solution.py:221
  43.8 26.7 %collective-permute-start.10 = (bf16[256,1024]{1,0:T(8,128)(2,1)}, bf16[256,1024]{1,0:T(8,128)(2,1)}, u32[]{:S(2)}, u32[]{:S(2)}) collective-permute-start(bf16[256,1024]{1,0:T(8,128)(2,1)} %refs_6_.3), channel_id=1, source_target_pairs={{0,1},{1,2},{2,3},{3,0},{4,5},{5,6},{6,7},{7,4},{8,9},{9,10},{10,1... | collective-permute-start | bytes 1572872 | tf_op jit(solution)/shard_map/ppermute | solution.py:221
  45.1 25.4 %collective-permute-start.9 = (bf16[256,256]{1,0:T(8,128)(2,1)}, bf16[256,256]{1,0:T(8,128)(2,1)S(1)}, u32[]{:S(2)}, u32[]{:S(2)}) collective-permute-start(bf16[256,256]{1,0:T(8,128)(2,1)} %slice.33), channel_id=1, source_target_pairs={{0,3},{1,0},{2,1},{3,2},{4,7},{5,4},{6,5},{7,6},{8,11},{9,8},{10,9... | collective-permute-start | bytes 393224 | tf_op jit(solution)/shard_map/ppermute | solution.py:221
  48.2 25.2 %collective-permute-start.8 = (bf16[256,256]{1,0:T(8,128)(2,1)S(1)}, bf16[256,256]{1,0:T(8,128)(2,1)S(1)}, u32[]{:S(2)}, u32[]{:S(2)}) collective-permute-start(bf16[256,256]{1,0:T(8,128)(2,1)S(1)} %slice.32), channel_id=1, source_target_pairs={{0,1},{1,2},{2,3},{3,0},{4,5},{5,6},{6,7},{7,4},{8,9},{9,10},{10,1... | collective-permute-start | bytes 393224 | tf_op jit(solution)/shard_map/ppermute | solution.py:221
  57.1 33.6 %collective-permute-start.16 = (bf16[256,256]{1,0:T(8,128)(2,1)S(1)}, bf16[256,256]{1,0:T(8,128)(2,1)S(1)}, u32[]{:S(2)}, u32[]{:S(2)}) collective-permute-start(bf16[256,256]{1,0:T(8,128)(2,1)S(1)} %slice.35), channel_id=1, source_target_pairs={{0,3},{1,0},{2,1},{3,2},{4,7},{5,4},{6,5},{7,6},{8,11},{9,8},{10,9... | collective-permute-start | bytes 393224 | tf_op jit(solution)/shard_map/ppermute | solution.py:221
  61.0 29.7 %collective-permute-start.15 = (bf16[256,256]{1,0:T(8,128)(2,1)S(1)}, bf16[256,256]{1,0:T(8,128)(2,1)S(1)}, u32[]{:S(2)}, u32[]{:S(2)}) collective-permute-start(bf16[256,256]{1,0:T(8,128)(2,1)S(1)} %slice.34), channel_id=1, source_target_pairs={{0,1},{1,2},{2,3},{3,0},{4,5},{5,6},{6,7},{7,4},{8,9},{9,10},{10,1... | collective-permute-start | bytes 393224 | tf_op jit(solution)/shard_map/ppermute | solution.py:221
  73.4 1.6 %copy-start.8 = (bf16[1024,1024]{1,0:T(8,128)(2,1)S(1)}, bf16[1024,1024]{1,0:T(8,128)(2,1)}, u32[]{:S(2)}) copy-start(bf16[1024,1024]{1,0:T(8,128)(2,1)} %refs_10_.3) | copy-start | bytes 6291460
  75.0 15.7 %copy-start.9 = (bf16[1024,1024]{1,0:T(8,128)(2,1)S(1)}, bf16[1024,1024]{1,0:T(8,128)(2,1)}, u32[]{:S(2)}) copy-start(bf16[1024,1024]{1,0:T(8,128)(2,1)} %refs_10_.3) | copy-start | bytes 6291460
  80.2 18.8 %collective-permute-start.17 = (bf16[256,512]{1,0:T(8,128)(2,1)S(1)}, bf16[256,512]{1,0:T(8,128)(2,1)S(1)}, u32[]{:S(2)}, u32[]{:S(2)}) collective-permute-start(bf16[256,512]{1,0:T(8,128)(2,1)S(1)} %pad_maximum_fusion.1), channel_id=1, source_target_pairs={{0,4},{4,8},{8,12},{12,16},{16,20},{20,24},{24,28},{28,32},{32,36}... | collective-permute-start | bytes 786440 | tf_op jit(solution)/shard_map/ppermute | solution.py:221
